TPU v7x, 256 devices: a whole 4x4x8 slice. The times are simulated.
256 devices in a mesh: coarse: 8 (over x, core), fine: 32 (over z, y).
Axes of the slice: x: 4, y: 4, z: 8, core: 2. Of those that a mesh axis runs over, the one named last changes fastest.
Arguments:
- tokens: bfloat16 [131072, 1024], P(('coarse', 'fine'))
- w_qkv: bfloat16 [1024, 3072], replicated, may hold values from -0.1875 to 0.1875
- w_coarse_out: bfloat16 [1024, 1024], replicated, may hold values from -0.1875 to 0.1875
- w_kv2: bfloat16 [1024, 2048], replicated, may hold values from -0.1875 to 0.1875
- w_out: bfloat16 [1024, 1024], replicated, may hold values from -0.1875 to 0.1875
- seg_start: int32 [4096], P('coarse'), may hold values from 0 to 131071, as said below
- seg_end: int32 [4096], P('coarse'), may hold values from 1 to 131072, as said below
- block_lists: int32 [512, 8], P(('coarse', 'fine')), may hold values from 0 to 255, as said below
Outputs:
- mixed: bfloat16 [131072, 1024], P(('coarse', 'fine'))
Inputs may be any that keep to these rules, and one draw needn't show every extreme that they name: `seg_start`: for each coarse owner c, the segments c*512 to (c+1)*512 - 1 are nonempty and pairwise disjoint and lie within time steps c*16384 to (c+1)*16384 - 1, listed in an order that does not follow time; steps outside all segments belong to none; segment lengths are uneven. seg_end[s] > seg_start[s]. `block_lists`: row n names 8 distinct coarse key blocks (block b holds segments b*16 to (b+1)*16 - 1), all among the blocks of owners c-1, c and c+1 taken cyclically over the owners, where c = n*256 // 16384 is the owner of the row's time steps.
All inputs are finite; a program needn't handle non-finite values.
Results may differ from a plain program's by a relative error of at most 0.017.
Values may be sent and summed in bfloat16 or wider, within the bound.
A program may use at most 128 MiB of HBM per device.

v0:
```python
import math

import jax
import jax.numpy as jnp
from jax import lax
from jax.sharding import PartitionSpec as P

HEADS = 8
KB = 16
QB = 256


def padded(cells, sides, width):
    for axis, dim in sides:
        count = lax.axis_size(axis)
        head = lax.slice_in_dim(cells, 0, width, axis=dim)
        tail = lax.slice_in_dim(cells, cells.shape[dim] - width, cells.shape[dim], axis=dim)
        cells = jnp.concatenate(
            [
                lax.ppermute(tail, axis, [(i, (i + 1) % count) for i in range(count)]),
                cells,
                lax.ppermute(head, axis, [((i + 1) % count, i) for i in range(count)]),
            ],
            axis=dim,
        )
    return cells


def attend_heads(queries, keys, content_elements, allowed):
    count = queries.shape[0]
    head_size = queries.shape[1] // HEADS
    query_heads = queries.reshape(count, HEADS, head_size)
    key_heads = keys.reshape(keys.shape[0], HEADS, head_size)
    value_heads = content_elements.reshape(content_elements.shape[0], HEADS, head_size)
    scores = jnp.einsum("qhd,khd->hqk", query_heads, key_heads, preferred_element_type=jnp.float32)
    scores = scores * (1.0 / math.sqrt(head_size))
    scores = jnp.where(allowed[None], scores, -1e30)
    highest = jnp.max(scores, axis=-1, keepdims=True)
    expos = jnp.exp(scores - highest)
    weights = (expos / jnp.sum(expos, axis=-1, keepdims=True)).astype(jnp.bfloat16)
    blended = jnp.einsum("hqk,khd->qhd", weights, value_heads, preferred_element_type=jnp.float32)
    return blended.astype(jnp.bfloat16).reshape(count, HEADS * head_size)


def normalize(content_elements):
    return content_elements * lax.rsqrt(
        jnp.mean(content_elements * content_elements, axis=-1, keepdims=True) + 1e-06
    )


def body(tokens, w_qkv, w_coarse_out, w_kv2, w_out, seg_start, seg_end, block_lists):
    rows_here = tokens.shape[0]
    width = tokens.shape[1]
    fine_count = lax.axis_size("fine")
    coarse_count = lax.axis_size("coarse")
    fine_index = lax.axis_index("fine")
    coarse_index = lax.axis_index("coarse")
    seg_owned = seg_start.shape[0]
    first_row = coarse_index * (rows_here * fine_count) + fine_index * rows_here
    positions = first_row + jnp.arange(rows_here, dtype=jnp.int32)
    member = (
        (positions[None, :] >= seg_start[:, None]) & (positions[None, :] < seg_end[:, None])
    ).astype(jnp.bfloat16)
    sums = lax.psum_scatter(
        jnp.dot(member, tokens, preferred_element_type=jnp.float32).astype(jnp.bfloat16),
        "fine",
        scatter_dimension=0,
        tiled=True,
    ).astype(jnp.float32)
    share_start = fine_index * KB
    spans = (
        lax.dynamic_slice_in_dim(seg_end, share_start, KB, 0)
        - lax.dynamic_slice_in_dim(seg_start, share_start, KB, 0)
    ).astype(jnp.float32)
    pooled = (sums / jnp.sqrt(spans)[:, None]).astype(jnp.bfloat16)
    coarse_proj = jnp.dot(pooled, w_qkv, preferred_element_type=jnp.float32)
    coarse_query = coarse_proj[:, :width].astype(jnp.bfloat16)
    coarse_pair = coarse_proj[:, width:].astype(jnp.bfloat16)
    owner_pairs = lax.all_gather(coarse_pair, "fine", axis=0, tiled=True)
    reach = seg_owned // 2
    window_table = padded(owner_pairs, (("coarse", 0),), reach)
    query_place = reach + share_start + jnp.arange(KB, dtype=jnp.int32)
    key_place = jnp.arange(window_table.shape[0], dtype=jnp.int32)
    allowed = jnp.abs(query_place[:, None] - key_place[None, :]) <= reach
    coarse_mix = attend_heads(
        coarse_query, window_table[:, :width], window_table[:, width:], allowed
    )
    context = jnp.dot(coarse_mix, w_coarse_out, preferred_element_type=jnp.float32)
    state = normalize(context).astype(jnp.bfloat16)
    payload = jnp.dot(state, w_kv2, preferred_element_type=jnp.float32).astype(jnp.bfloat16)
    seg_total = seg_owned * coarse_count
    owner_rows = lax.all_gather(payload, "fine", axis=0, tiled=True)
    second_table = padded(owner_rows, (("coarse", 0),), seg_owned)
    table_base = (coarse_index - 1) * seg_owned
    proj = jnp.dot(tokens, w_qkv, preferred_element_type=jnp.float32)
    query = proj[:, :width].astype(jnp.bfloat16)
    key_rows = proj[:, width : 2 * width].astype(jnp.bfloat16)
    value_rows = proj[:, 2 * width :].astype(jnp.bfloat16)
    listed_rows = (
        block_lists[:, :, None] * KB + jnp.arange(KB, dtype=jnp.int32)[None, None, :]
    ).reshape(block_lists.shape[0], -1)
    table_rows = jnp.mod(listed_rows - table_base, seg_total)
    block_rows = min(512, rows_here)
    sub_blocks = block_rows // QB
    remote_per_sub = table_rows.shape[1]
    query_group = jnp.arange(block_rows, dtype=jnp.int32) // QB
    remote_group = jnp.arange(sub_blocks * remote_per_sub, dtype=jnp.int32) // remote_per_sub
    allowed_fine = jnp.concatenate(
        [
            jnp.ones((block_rows, rows_here), dtype=bool),
            query_group[:, None] == remote_group[None, :],
        ],
        axis=1,
    )

    def query_block(number):
        wanted = table_rows.reshape(-1)
        remote = jnp.take(second_table, wanted, axis=0)
        keys = jnp.concatenate([key_rows, remote[:, :width]], axis=0)
        content_elements = jnp.concatenate([value_rows, remote[:, width:]], axis=0)
        return attend_heads(query, keys, content_elements, allowed_fine)

    attended = lax.map(query_block, jnp.arange(rows_here // block_rows, dtype=jnp.int32)).reshape(
        rows_here, width
    )
    projected = jnp.dot(attended, w_out, preferred_element_type=jnp.float32)
    return normalize(projected).astype(jnp.bfloat16)


def solution(mesh):
    placed = (
        P(("coarse", "fine"), None),
        P(),
        P(),
        P(),
        P(),
        P("coarse"),
        P("coarse"),
        P(("coarse", "fine"), None),
    )
    return jax.shard_map(
        body, mesh=mesh, in_specs=placed, out_specs=P(("coarse", "fine"), None), check_vma=False
    )
```

profile of v0, /device:TPU:1, one launch (start us, length us, event | category | flops | bytes accessed | tf_op | source)
XLA Modules:
  0.0 506.6 jit_solution(6676271423048525589)
XLA Ops:
  6.5 0.0 copy-start
  6.5 0.0 reduce-scatter.2.cloned.1.call-start
  6.5 3.1 convolution_convert_fusion.3
  9.7 0.0 reduce-scatter.2.cloned.1.call-update
  9.7 0.0 all-gather.3.cloned.1.call-start
  9.8 0.8 convert_sqrt_fusion
  10.5 215.7 %reduce-scatter.2.cloned.1.call-done = bf16[16,1024]{1,0:T(8,128)(2,1)} async-done(((bf16[512,1024]{1,0:T(8,128)(2,1)}), bf16[16,1024]{1,0:T(8,128)(2,1)}) %reduce-scatter.2.cloned.1.call-update) | async-done | bytes 32784 | tf_op jit(solution)/shard_map/reduce_scatter | solution.py:64
  226.3 3.8 convolution_convert_fusion.1
  230.0 0.6 slice.55
  230.7 0.0 all-gather.3.cloned.1.call-update
  230.7 0.0 all-gather.5.cloned.1.call-start
  230.7 77.0 %all-gather.3.cloned.1.call-done = bf16[512,2048]{1,0:T(8,128)(2,1)} async-done(((bf16[16,2048]{1,0:T(8,128)(2,1)}), bf16[512,2048]{1,0:T(8,128)(2,1)}) %all-gather.3.cloned.1.call-update) | async-done | bytes 2097168 | tf_op jit(solution)/shard_map/all_gather | solution.py:79
  307.7 3.1 fusion.55
  310.8 6.5 %collective-permute-start = (bf16[256,2048]{1,0:T(8,128)(2,1)}, bf16[256,2048]{1,0:T(8,128)(2,1)}, u32[]{:S(2)}, u32[]{:S(2)}) collective-permute-start(bf16[256,2048]{1,0:T(8,128)(2,1)} %get-tuple-element.34), channel_id=1, source_target_pairs={{0,32},{32,64},{64,96},{96,128},{128,160},{160,192},{192,224},{224... | collective-permute-start | bytes 3145736 | tf_op jit(solution)/shard_map/ppermute | solution.py:20
  317.4 0.0 collective-permute-start.1
  317.4 0.0 copy-start.1
  317.4 0.1 abs_compare_fusion
  317.5 12.0 %collective-permute-done = bf16[256,2048]{1,0:T(8,128)(2,1)} collective-permute-done((bf16[256,2048]{1,0:T(8,128)(2,1)}, bf16[256,2048]{1,0:T(8,128)(2,1)}, u32[]{:S(2)}, u32[]{:S(2)}) %collective-permute-start) | collective-permute-done | bytes 1048608 | tf_op jit(solution)/shard_map/ppermute | solution.py:20
  329.4 1.3 constant_dynamic-update-slice_fusion.2
  330.8 0.0 copy-done.1
  330.8 0.1 constant_dynamic-update-slice_fusion.1
  330.9 0.9 collective-permute-done.1
  331.8 0.1 constant_dynamic-update-slice_fusion
  331.9 2.9 slice_bitcast_fusion.1
  334.8 2.4 fusion.57
  337.2 0.0 copy-start.2
  337.2 2.4 fusion.28
  339.6 0.0 copy-start.7
  339.6 2.1 multiply_reduce_fusion.1
  341.7 0.0 copy-done.2
  341.7 1.3 convolution_convert_fusion.2
  343.0 0.0 all-gather.5.cloned.1.call-update
  343.1 0.0 copy-done.7
  343.1 0.1 add.149
  343.2 0.1 add.167
  343.2 0.1 add.150
  343.3 0.1 add.152
  343.4 70.0 %all-gather.5.cloned.1.call-done = bf16[512,2048]{1,0:T(8,128)(2,1)} async-done(((bf16[16,2048]{1,0:T(8,128)(2,1)}), bf16[512,2048]{1,0:T(8,128)(2,1)}) %all-gather.5.cloned.1.call-update) | async-done | bytes 2097168 | tf_op jit(solution)/shard_map/all_gather | solution.py:92
  413.4 5.5 %collective-permute-start.3 = (bf16[512,2048]{1,0:T(8,128)(2,1)}, bf16[512,2048]{1,0:T(8,128)(2,1)S(1)}, u32[]{:S(2)}, u32[]{:S(2)}) collective-permute-start(bf16[512,2048]{1,0:T(8,128)(2,1)} %all-gather.5.cloned.1.call-done), channel_id=1, source_target_pairs={{32,0},{64,32},{96,64},{128,96},{160,128},{192,160},{224,192},{0,2... | collective-permute-start | bytes 6291464 | tf_op jit(solution)/shard_map/ppermute | solution.py:22
  418.9 1.1 collective-permute-start.2
  420.0 0.1 broadcast_compare_fusion
  420.2 0.1 concatenate.20
  420.3 6.5 %convolution_convert_fusion = bf16[512,3072]{1,0:T(8,128)(2,1)S(1)} fusion(bf16[512,1024]{1,0:T(8,128)(2,1)} %param.8, bf16[1024,3072]{1,0:T(8,128)(2,1)} %param.9), kind=kOutput, calls=%fused_computation.12 | convolution fusion | flops 3222798336 | bytes 10485760 | tf_op jit(solution)/shard_map/dot_general | solution.py:95
  426.9 0.0 copy-start.5
  426.9 1.8 slice_bitcast_fusion.2
  428.6 15.6 %collective-permute-done.3 = bf16[512,2048]{1,0:T(8,128)(2,1)S(1)} collective-permute-done((bf16[512,2048]{1,0:T(8,128)(2,1)}, bf16[512,2048]{1,0:T(8,128)(2,1)S(1)}, u32[]{:S(2)}, u32[]{:S(2)}) %collective-permute-start.3) | collective-permute-done | bytes 2097184 | tf_op jit(solution)/shard_map/ppermute | solution.py:22
  444.2 0.0 collective-permute-done.2
  444.2 0.0 copy-done.5
  444.2 11.2 %pad_maximum_fusion = bf16[1536,2048]{1,0:T(8,128)(2,1)} fusion(bf16[512,2048]{1,0:T(8,128)(2,1)S(1)} %collective-permute-done.3, bf16[512,2048]{1,0:T(8,128)(2,1)S(1)} %copy-done.5, bf16[512,2048]{1,0:T(8,128)(2,1)S(1)} %collective-permute-done.2), kind=kLoop, calls=%fused_computation.7 | loop fusion | flops 18874368 | bytes 12582912 | tf_op jit(solution)/shard_map/concatenate | solution.py:18
  455.4 6.0 %gather_fusion = bf16[256,2048]{1,0:T(8,128)(2,1)S(1)} fusion(bf16[1536,2048]{1,0:T(8,128)(2,1)} %pad_maximum_fusion, s32[1024]{0:T(1024)S(1)} %pad_clamp_fusion), kind=kCustom, calls=%fused_computation | custom fusion | bytes 2098176 | tf_op jit(solution)/shard_map/while/body/eval_jaxpr/jit(_take)/gather | solution.py:118
  461.4 0.0 copy-start.3
  461.4 0.2 broadcast_select_fusion
  461.6 0.9 fusion.56
  462.4 0.3 copy-done.3
  462.7 1.3 pad_maximum_fusion.1
  464.0 2.6 copy.22
  466.6 0.0 copy-done.4
  466.6 7.7 %fusion.13 = f32[8,512,768]{2,1,0:T(8,128)} fusion(bf16[64,8,8,128]{3,2,1,0:T(8,128)(2,1)S(1)} %copy-done.4, bf16[256,1024]{1,0:T(8,128)(2,1)} %get-tuple-element.36, bf16[512,1024]{1,0:T(8,128)(2,1)} %get-tuple-element.22), kind=kOutput, calls=%fused_computation.25 | convolution fusion | flops 808452096 | bytes 15204352 | tf_op jit(solution)/shard_map/while/body/eval_jaxpr/qhd,khd->hqk/dot_general | solution.py:35
  474.3 16.3 %fusion.58 = (f32[8,512]{1,0:T(8,128)S(1)}, f32[8,512,768]{2,1,0:T(8,128)}) fusion(f32[8,512,768]{2,1,0:T(8,128)} %fusion.13, pred[512,768]{1,0:T(8,128)(4,1)S(1)} %concatenate.20), kind=kOutput, calls=%fused_computation.102 | output fusion | flops 18875136 | bytes 25575424 | tf_op jit(solution)/shard_map/while/body/eval_jaxpr/sub | solution.py:39
  490.7 0.0 copy-done.6
  490.7 6.9 %fusion.16 = bf16[8,128,512]{2,1,0:T(8,128)(2,1)S(1)} fusion(bf16[768,8,128]{0,2,1:T(8,128)(2,1)S(1)} %bitcast.73, f32[8,512,768]{2,1,0:T(8,128)} %get-tuple-element.43, f32[8,512]{1,0:T(8,128)S(1)} %get-tuple-element.42), kind=kOutput, calls=%fused_computation.31 | convolution fusion | flops 812122112 | bytes 15220736 | tf_op jit(solution)/shard_map/while/body/eval_jaxpr/hqk,khd->qhd/dot_general | solution.py:41
  497.5 0.0 copy-done
  497.5 1.4 multiply_reduce_fusion
  498.9 1.2 multiply_convert_fusion
  (14 shorter events, 0.1 us)
Async XLA Ops:
  6.5 491.0 %copy-start = (bf16[1024,1024]{1,0:T(8,128)(2,1)S(1)}, bf16[1024,1024]{1,0:T(8,128)(2,1)}, u32[]{:S(2)}) copy-start(bf16[1024,1024]{1,0:T(8,128)(2,1)} %param.12) | copy-start | bytes 6291460
  6.5 219.7 %reduce-scatter.2.cloned.1.call-start = ((), (), s32[]{:S(2)}) async-start(), calls=%async_computation.1 | async-start | bytes 1081344 | tf_op jit(solution)/shard_map/reduce_scatter | solution.py:64
  9.7 298.0 %all-gather.3.cloned.1.call-start = ((), (), s32[]{:S(2)}) async-start(), calls=%async_computation.2 | async-start | bytes 2162688 | tf_op jit(solution)/shard_map/all_gather | solution.py:79
  230.7 182.8 %all-gather.5.cloned.1.call-start = ((), (), s32[]{:S(2)}) async-start(), calls=%async_computation.3 | async-start | bytes 2162688 | tf_op jit(solution)/shard_map/all_gather | solution.py:92
  310.8 18.6 %collective-permute-start = (bf16[256,2048]{1,0:T(8,128)(2,1)}, bf16[256,2048]{1,0:T(8,128)(2,1)}, u32[]{:S(2)}, u32[]{:S(2)}) collective-permute-start(bf16[256,2048]{1,0:T(8,128)(2,1)} %get-tuple-element.34), channel_id=1, source_target_pairs={{0,32},{32,64},{64,96},{96,128},{128,160},{160,192},{192,224},{224... | collective-permute-start | bytes 3145736 | tf_op jit(solution)/shard_map/ppermute | solution.py:20
  317.4 14.4 %collective-permute-start.1 = (bf16[256,2048]{1,0:T(8,128)(2,1)}, bf16[256,2048]{1,0:T(8,128)(2,1)S(1)}, u32[]{:S(2)}, u32[]{:S(2)}) collective-permute-start(bf16[256,2048]{1,0:T(8,128)(2,1)} %get-tuple-element.32), channel_id=1, source_target_pairs={{32,0},{64,32},{96,64},{128,96},{160,128},{192,160},{224,192},{0,2... | collective-permute-start | bytes 3145736 | tf_op jit(solution)/shard_map/ppermute | solution.py:22
  317.4 13.4 %copy-start.1 = (bf16[512,2048]{1,0:T(8,128)(2,1)S(1)}, bf16[512,2048]{1,0:T(8,128)(2,1)}, u32[]{:S(2)}) copy-start(bf16[512,2048]{1,0:T(8,128)(2,1)} %all-gather.3.cloned.1.call-done) | copy-start | bytes 6291460
  337.2 4.5 copy-start.2
  339.6 3.5 copy-start.7
  413.4 30.8 %collective-permute-start.3 = (bf16[512,2048]{1,0:T(8,128)(2,1)}, bf16[512,2048]{1,0:T(8,128)(2,1)S(1)}, u32[]{:S(2)}, u32[]{:S(2)}) collective-permute-start(bf16[512,2048]{1,0:T(8,128)(2,1)} %all-gather.5.cloned.1.call-done), channel_id=1, source_target_pairs={{32,0},{64,32},{96,64},{128,96},{160,128},{192,160},{224,192},{0,2... | collective-permute-start | bytes 6291464 | tf_op jit(solution)/shard_map/ppermute | solution.py:22
  418.9 25.3 %collective-permute-start.2 = (bf16[512,2048]{1,0:T(8,128)(2,1)}, bf16[512,2048]{1,0:T(8,128)(2,1)S(1)}, u32[]{:S(2)}, u32[]{:S(2)}) collective-permute-start(bf16[512,2048]{1,0:T(8,128)(2,1)} %all-gather.5.cloned.1.call-done), channel_id=1, source_target_pairs={{0,32},{32,64},{64,96},{96,128},{128,160},{160,192},{192,224},{224... | collective-permute-start | bytes 6291464 | tf_op jit(solution)/shard_map/ppermute | solution.py:20
  426.9 17.3 %copy-start.5 = (bf16[512,2048]{1,0:T(8,128)(2,1)S(1)}, bf16[512,2048]{1,0:T(8,128)(2,1)}, u32[]{:S(2)}) copy-start(bf16[512,2048]{1,0:T(8,128)(2,1)} %all-gather.5.cloned.1.call-done) | copy-start | bytes 6291460
  461.4 1.3 copy-start.3
  462.7 3.9 copy-start.4
  474.3 16.3 %copy-start.6 = (bf16[768,1024]{0,1:T(8,128)(2,1)S(1)}, bf16[768,1024]{0,1:T(8,128)(2,1)}, u32[]{:S(2)}) copy-start(bf16[768,1024]{0,1:T(8,128)(2,1)} %copy.22) | copy-start | bytes 4718596
Sparse Core Ops, SparseCore 0:
  11.1 215.0 reduce-scatter.1
  230.8 76.8 all-gather.2
  343.2 70.2 all-gather.4
where the time goes:
time: 507 us
  waiting for transfers between devices  391 us (77%)
  matrix products  37.7 us (7%)
  other arithmetic  31.2 us (6%)
  local copies, waits for them, and re-layouts  20.1 us (4%)
  between operations  13.3 us (3%)
  starting transfers between devices  13.2 us (3%)
    reduce_scatter x1, waiting for transfers between devices, body(): lax.psum_scatter(jnp.dot(member, tokens, preferred_element_type=jnp.float...  216 us
    all_gather x1, waiting for transfers between devices, body(): owner_pairs = lax.all_gather(coarse_pair, 'fine', axis=0, tiled=True)  77 us
    all_gather x1, waiting for transfers between devices, body(): owner_rows = lax.all_gather(payload, 'fine', axis=0, tiled=True)  70 us
    ppermute x2, waiting for transfers between devices, padded(): lax.ppermute(head, axis, [((i + 1) % count, i) for i in range(count)])  16.5 us
    sub x1, other arithmetic, attend_heads(): expos = jnp.exp(scores - highest)  16.3 us
    ppermute x2, waiting for transfers between devices, padded(): lax.ppermute(tail, axis, [(i, (i + 1) % count) for i in range(count)])  12 us
    concatenate x1, other arithmetic, padded(): jnp.concatenate([lax.ppermute(tail, axis, [(i, (i + 1) % count) for i in...  11.2 us
  transfers between devices with their start and end apart: 7, of which 6 were waited for; matrix products, arithmetic and copies ran while one was open for 2% of the time, Pallas kernels for 0%

commit v1 on v0

v1 whole, which is shorter than its diff:
```python
import math

import jax
import jax.numpy as jnp
from jax import lax
from jax.experimental import pallas as pl
from jax.experimental.pallas import tpu as pltpu
from jax.sharding import PartitionSpec as P

HEADS = 8
KB = 16
QB = 256
NY = 4
NZ = 8
NC = 8
D = 1024
HS = 128
ROWS = 512
SEGS = 512
REACH = 256
SCALE = 1.0 / math.sqrt(HS)
SCALE2 = SCALE * math.log2(math.e)
BF = jnp.bfloat16
F32 = jnp.float32
NT = (((1,), (1,)), ((), ()))
MESH = pl.DeviceIdType.MESH


def dot(a, b):
    return jnp.dot(a, b, preferred_element_type=F32)


def dot_nt(a, b):
    return lax.dot_general(a, b, NT, preferred_element_type=F32)


def normalize(x):
    return x * lax.rsqrt(jnp.mean(x * x, axis=-1, keepdims=True) + 1e-06)


def kernel(
    seg_ref, pick_ref, tok_hbm, wqkv_hbm, wco_hbm, wkv2_hbm, wout_hbm, out_ref,
    tok, wqkv, wco, wkv2, wout, part, ra, rb, sab, r2, red, rz, t1, t2, qkv, acc, mloc, lloc,
    qk, gath, kv2, att, load_sem, send_sem, recv_sem,
):
    c = lax.axis_index("coarse")
    f = lax.axis_index("fine")
    z = f // NY
    y = f % NY
    ya = y + 1 - 2 * (y % 2)
    yb = 3 - y
    yc = (y + 2) % 4
    up = (c + 1) % NC
    down = (c + NC - 1) % NC

    loads = [
        pltpu.make_async_copy(src, dst, load_sem.at[i])
        for i, (src, dst) in enumerate(
            ((tok_hbm, tok), (wqkv_hbm, wqkv), (wco_hbm, wco), (wkv2_hbm, wkv2), (wout_hbm, wout))
        )
    ]
    for load in loads:
        load.start()

    at_y = lambda yy: {"fine": z * NY + yy}
    at_z = lambda zz: {"fine": zz * NY + y}
    at_c = lambda cc: {"coarse": cc}

    barrier = pltpu.get_barrier_semaphore()
    peers = [at_z((z + dz) % NZ) for dz in range(1, NZ)]
    peers += [at_y(ya), at_y(yb), at_c(up), at_c(down)]
    for peer in peers:
        pl.semaphore_signal(barrier, inc=1, device_id=peer, device_id_type=MESH)

    counter = [0]

    def send(src, dst, where):
        k = counter[0]
        counter[0] = k + 1
        copy = pltpu.make_async_remote_copy(
            src_ref=src, dst_ref=dst, send_sem=send_sem.at[k], recv_sem=recv_sem.at[k],
            device_id=where, device_id_type=MESH,
        )
        copy.start()
        copies.append(copy)
        return copy

    copies = []
    first_row = (c * (NY * NZ) + f) * ROWS

    def partial(yy):
        rows = pl.ds(pl.multiple_of(yy * 128, 128), 128)
        low = seg_ref[rows, 0:1] - first_row
        high = seg_ref[rows, 1:2] - first_row
        place = lax.broadcasted_iota(jnp.int32, (128, ROWS), 1)
        member = jnp.where((place >= low) & (place < high), 1.0, 0.0).astype(BF)
        part[yy] = dot(member, tok[...]).astype(BF).reshape(NZ, KB, D)

    lo = pl.ds(0, 4)
    hi = pl.ds(4, 4)
    loads[0].wait()
    partial(yc)
    pl.semaphore_wait(barrier, len(peers))
    a1 = send(part.at[yc, lo], ra.at[1], at_y(ya))
    b1 = send(part.at[yc, hi], rb.at[1], at_y(yb))
    partial(ya)
    a0 = send(part.at[ya, lo], ra.at[0], at_y(ya))
    partial(yb)
    b0 = send(part.at[yb, hi], rb.at[0], at_y(yb))
    partial(y)

    def project(j, carry):
        cols = pl.ds(pl.multiple_of(j * 256, 256), 256)
        qkv[:, cols] = dot(tok[...], wqkv[:, cols]).astype(BF)
        return carry

    loads[1].wait()
    lax.fori_loop(0, 6, project, 0)

    a1.wait_recv()
    sab[0] = (part[yb, 0:4].astype(F32) + ra[1].astype(F32)).astype(BF)
    a2 = send(sab.at[0], r2.at[0], at_y(yb))
    b1.wait_recv()
    sab[1] = (part[ya, 4:8].astype(F32) + rb[1].astype(F32)).astype(BF)
    b2 = send(sab.at[1], r2.at[1], at_y(ya))
    lax.fori_loop(6, 12, project, 0)
    a0.wait_recv()
    a2.wait_recv()
    red[0:4] = (part[y, 0:4].astype(F32) + ra[0].astype(F32) + r2[0].astype(F32)).astype(BF)
    b0.wait_recv()
    b2.wait_recv()
    red[4:8] = (part[y, 4:8].astype(F32) + rb[0].astype(F32) + r2[1].astype(F32)).astype(BF)
    order = (4, 3, 5, 2, 6, 1, 7)
    zs = [send(red.at[(z + dz) % NZ], rz.at[dz - 1], at_z((z + dz) % NZ)) for dz in order]

    def local(it, carry):
        rows = pl.ds(pl.multiple_of((it // HEADS) * QB, QB), QB)
        col = (it % HEADS) * HS
        cols = pl.ds(pl.multiple_of(col, HS), HS)
        keys = qkv[:, pl.ds(pl.multiple_of(col + D, HS), HS)]
        vals = qkv[:, pl.ds(pl.multiple_of(col + 2 * D, HS), HS)]
        s = dot_nt(qkv[rows, cols], keys)
        m = jnp.max(s, axis=1, keepdims=True)
        p = jnp.exp2((s - m) * SCALE2)
        lloc[it] = jnp.sum(p, axis=1, keepdims=True)
        mloc[it] = m
        acc[rows, cols] = dot(p.astype(BF), vals)
        return carry

    lax.fori_loop(0, 8, local, 0)

    for copy in zs:
        copy.wait_recv()
    total = red[z].astype(F32)
    for dz in range(1, NZ):
        total = total + rz[dz - 1].astype(F32)
    mine = seg_ref[pl.ds(pl.multiple_of((y * NZ + z) * KB, KB), KB), :]
    span = (mine[:, 1:2] - mine[:, 0:1]).astype(F32)
    pooled = (total / jnp.sqrt(span)).astype(BF)
    t1[4 + z, y] = pooled

    def gather(table, base, own_first, work):
        zc = [
            send(table.at[base + z, y], table.at[base + z, y], at_z((z + dz) % NZ)) for dz in order
        ]
        work[0]()
        for copy in zc:
            copy.wait_recv()
        low = pl.ds(base, 4)
        high = pl.ds(base + 4, 4)
        ups = high if own_first else pl.ds(base, 8)
        downs = low if own_first else pl.ds(base, 8)
        size = 4 if own_first else 8
        top = 12 if own_first else 16
        halo = []

        def to_owners(yy):
            halo.append(send(table.at[ups, yy], table.at[pl.ds(0, size), yy], at_c(up)))
            halo.append(send(table.at[downs, yy], table.at[pl.ds(top, size), yy], at_c(down)))

        y1 = send(table.at[low, y], table.at[low, y], at_y(ya))
        y2 = send(table.at[high, y], table.at[high, y], at_y(yb))
        y3 = send(table.at[low, y], table.at[low, y], at_y(yb))
        y4 = send(table.at[high, y], table.at[high, y], at_y(ya))
        to_owners(y)
        work[1]()
        y1.wait_recv()
        y5 = send(table.at[low, ya], table.at[low, ya], at_y(yb))
        y2.wait_recv()
        y6 = send(table.at[high, yb], table.at[high, yb], at_y(ya))
        y4.wait_recv()
        to_owners(ya)
        y3.wait_recv()
        to_owners(yb)
        y5.wait_recv()
        y6.wait_recv()
        to_owners(yc)
        work[2]()
        for copy in halo:
            copy.wait_recv()

    def absorb():
        query = dot(pooled, wqkv[:, 0:D]).astype(BF)
        for h in range(HEADS):
            qk[h * KB:(h + 1) * KB] = dot_nt(
                query[:, h * HS:(h + 1) * HS], wqkv[:, D + h * HS:D + (h + 1) * HS]
            ).astype(BF)

    gather(
        t1, 4, True,
        (absorb, lambda: lax.fori_loop(8, 12, local, 0), lambda: lax.fori_loop(12, 16, local, 0)),
    )

    table = t1[...].reshape(1024, D)
    s = dot_nt(qk[...], table)
    row = lax.broadcasted_iota(jnp.int32, s.shape, 0) % KB + f * KB
    key = lax.broadcasted_iota(jnp.int32, s.shape, 1) - REACH
    s = jnp.where(jnp.abs(row - key) <= REACH, s, -1e30)
    m = jnp.max(s, axis=1, keepdims=True)
    p = jnp.exp2((s - m) * SCALE2)
    w = (p / jnp.sum(p, axis=1, keepdims=True)).astype(BF)
    mixed = dot(w, table).astype(BF)
    mix = jnp.concatenate(
        [
            dot(mixed[h * KB:(h + 1) * KB], wqkv[:, 2 * D + h * HS:2 * D + (h + 1) * HS])
            for h in range(HEADS)
        ],
        axis=1,
    ).astype(BF)
    loads[2].wait()
    state = normalize(dot(mix, wco[...])).astype(BF)
    t2[8 + z, y] = state
    nothing = lambda: None
    gather(t2, 8, False, (nothing, nothing, nothing))

    for j in range(16):
        idx = pick_ref[j]
        gath[j * KB:(j + 1) * KB] = t2[idx // NY, idx % NY]
    loads[3].wait()

    def second(j, carry):
        cols = pl.ds(pl.multiple_of(j * 256, 256), 256)
        kv2[:, cols] = dot(gath[...], wkv2[:, cols]).astype(BF)
        return carry

    lax.fori_loop(0, 8, second, 0)

    def remote(it, carry):
        n = it // HEADS
        rows = pl.ds(pl.multiple_of(n * QB, QB), QB)
        col = (it % HEADS) * HS
        cols = pl.ds(pl.multiple_of(col, HS), HS)
        listed = pl.ds(pl.multiple_of(n * 128, 128), 128)
        s = dot_nt(qkv[rows, cols], kv2[listed, cols])
        m0 = mloc[it]
        m = jnp.maximum(m0, jnp.max(s, axis=1, keepdims=True))
        a = jnp.exp2((m0 - m) * SCALE2)
        p = jnp.exp2((s - m) * SCALE2)
        total = a * lloc[it] + jnp.sum(p, axis=1, keepdims=True)
        vals = kv2[listed, pl.ds(pl.multiple_of(col + D, HS), HS)]
        o = acc[rows, cols] * a + dot(p.astype(BF), vals)
        att[rows, cols] = (o / total).astype(BF)
        return carry

    lax.fori_loop(0, 16, remote, 0)
    loads[4].wait()

    def finish(i, carry):
        rows = pl.ds(pl.multiple_of(i * 128, 128), 128)
        out_ref[rows, :] = normalize(dot(att[rows, :], wout[...])).astype(BF)
        return carry

    lax.fori_loop(0, 4, finish, 0)
    for copy in copies:
        copy.wait_send()


COPIES = 4 + 2 + 7 + 2 * (7 + 6 + 8)


def body(tokens, w_qkv, w_coarse_out, w_kv2, w_out, seg_start, seg_end, block_lists):
    seg = jnp.stack([seg_start, seg_end], axis=1).reshape(NZ, NY, KB, 2)
    seg = seg.transpose(1, 0, 2, 3).reshape(SEGS, 2)
    base = (lax.axis_index("coarse") - 1) * (SEGS // KB)
    pick = jnp.mod(block_lists.reshape(-1) - base, NC * SEGS // KB)
    vmem = lambda shape, kind: pltpu.VMEM(shape, kind)
    return pl.pallas_call(
        kernel,
        out_shape=jax.ShapeDtypeStruct((ROWS, D), BF),
        in_specs=[
            pl.BlockSpec(memory_space=pltpu.VMEM),
            pl.BlockSpec(memory_space=pltpu.SMEM),
        ] + [pl.BlockSpec(memory_space=pl.ANY)] * 5,
        out_specs=pl.BlockSpec(memory_space=pltpu.VMEM),
        scratch_shapes=[
            vmem((ROWS, D), BF),
            vmem((D, 3 * D), BF),
            vmem((D, D), BF),
            vmem((D, 2 * D), BF),
            vmem((D, D), BF),
            vmem((NY, NZ, KB, D), BF),
            vmem((2, 4, KB, D), BF),
            vmem((2, 4, KB, D), BF),
            vmem((2, 4, KB, D), BF),
            vmem((2, 4, KB, D), BF),
            vmem((NZ, KB, D), BF),
            vmem((NZ - 1, KB, D), BF),
            vmem((16, NY, KB, D), BF),
            vmem((24, NY, KB, D), BF),
            vmem((ROWS, 3 * D), BF),
            vmem((ROWS, D), F32),
            vmem((16, QB, 1), F32),
            vmem((16, QB, 1), F32),
            vmem((HEADS * KB, D), BF),
            vmem((256, D), BF),
            vmem((256, 2 * D), BF),
            vmem((ROWS, D), BF),
            pltpu.SemaphoreType.DMA((5,)),
            pltpu.SemaphoreType.DMA((COPIES,)),
            pltpu.SemaphoreType.DMA((COPIES,)),
        ],
        compiler_params=pltpu.CompilerParams(
            collective_id=0, has_side_effects=True, vmem_limit_bytes=60 * 1024 * 1024
        ),
    )(seg, pick, tokens, w_qkv, w_coarse_out, w_kv2, w_out)


def solution(mesh):
    placed = (
        P(("coarse", "fine"), None),
        P(),
        P(),
        P(),
        P(),
        P("coarse"),
        P("coarse"),
        P(("coarse", "fine"), None),
    )
    return jax.shard_map(
        body, mesh=mesh, in_specs=placed, out_specs=P(("coarse", "fine"), None), check_vma=False
    )
```

time: 507 us -> 97.1 us (0.19)
  waiting for transfers between devices: 391 us -> 0 us
  Pallas kernels: 0 us -> 90.4 us
  matrix products: 37.7 us -> 0 us
  other arithmetic: 31.2 us -> 1.29 us
  local copies, waits for them, and re-layouts: 20.1 us -> 4.85 us
  between operations: 13.3 us -> 0.02 us
  starting transfers between devices: 13.2 us -> 0 us
    reduce_scatter x1 -> x0, waiting for transfers between devices: 216 us -> none  [body(): lax.psum_scatter(jnp.dot(member, tokens, preferred_element_type=jnp.float...]
    all_gather x2 -> x0, waiting for transfers between devices: 147 us -> none  [the longest x1 77 us: body(): owner_pairs = lax.all_gather(coarse_pair, 'fine', axis=0, tiled=True)]
    pallas_call x0 -> x1, Pallas kernels: none -> 90.4 us  [body(): pl.pallas_call(kernel, out_shape=jax.ShapeDtypeStruct((ROWS, D), BF), in_...]
    dot_general x9 -> x0, matrix products: 35.2 us -> none  [the longest x2 9.22 us: attend_heads(): jnp.einsum('hqk,khd->qhd', weights, value_heads, preferred_element_type=j...]
    ppermute x4 -> x0, waiting for transfers between devices: 28.4 us -> none  [the longest x2 16.5 us: padded(): lax.ppermute(head, axis, [((i + 1) % count, i) for i in range(count)])]
    sub x1, other arithmetic: 16.3 us -> 0.68 us  [body(): pick = jnp.mod(block_lists.reshape(-1) - base, NC * SEGS // KB)]
    ppermute x4 -> x0, starting transfers between devices: 13.1 us -> none  [the longest x2 7.62 us: padded(): lax.ppermute(tail, axis, [(i, (i + 1) % count) for i in range(count)])]
    concatenate x2 -> x0, other arithmetic: 12.4 us -> none  [the longest x1 11.2 us: padded(): jnp.concatenate([lax.ppermute(tail, axis, [(i, (i + 1) % count) for i in...]
  transfers between devices with their start and end apart: 7 -> 0, of which waited for: 6 -> 0; matrix products, arithmetic and copies ran while one was open for 2% -> 0% of each run, Pallas kernels for 0% -> 0%
where the time goes in v1:
time: 97.1 us; the launch traced here: 96.5 us
  Pallas kernels  90.4 us (93%)
  local copies, waits for them, and re-layouts  4.85 us (5%)
  other arithmetic  1.29 us (1%)
    pallas_call x1, Pallas kernels, body(): pl.pallas_call(kernel, out_shape=jax.ShapeDtypeStruct((ROWS, D), BF), in_...  90.4 us
    unnamed x1, local copies, waits for them, and re-layouts  2.26 us

profile of v1, /device:TPU:1, one launch (start us, length us, event | category | flops | bytes accessed | tf_op | source)
XLA Modules:
  0.0 96.5 jit_solution(16078165253137163042)
XLA Ops:
  0.0 0.7 broadcast_subtract_fusion
  0.7 0.1 sub.15
  0.8 0.6 and_select_fusion.pick_ref
  1.4 0.8 stack.9
  2.1 0.8 stack.10
  2.9 1.0 %copy.9 = s32[4,8,16,2]{3,2,1,0:T(8,128)} copy(s32[4,8,16,2]{2,0,1,3:T(4,128)S(1)} %add_bitcast_fusion) | data formatting | bytes 8192 | tf_op jit(solution)/shard_map/transpose | solution.py:283
  3.9 90.4 %shard_map.82 = bf16[512,1024]{1,0:T(8,128)(2,1)} custom-call(s32[512,2]{1,0:T(8,128)} %bitcast.3, s32[16]{0:T(128)} %and_select_fusion.pick_ref, bf16[512,1024]{1,0:T(8,128)(2,1)} %tok_hbm.1, bf16[1024,3072]{1,0:T(8,128)(2,1)} %wqkv_hbm.1, bf16[1024,1024]{1,0:T(8,128)(2,1)} %wco_hbm.1, bf16[1024,2048]{1,0:T(8,128)(2,1)} %wkv2_hbm.1, bf16[1024,1024]{1,0:T(8,128)(2,1)} %wout_hbm.1), custom_call_target="tpu_custom_call" | custom-call | tf_op jit(solution)/shard_map/pallas_call | solution.py:287
  94.3 2.3 %copy.11 = bf16[512,1024]{1,0:T(8,128)(2,1)} copy(bf16[512,1024]{1,0:T(8,128)(2,1)} %shard_map.82) | data formatting | bytes 2097152
  (1 shorter events, 0.0 us)

commit v2 on v1

v2 whole, which is shorter than its diff:
```python
import math

import jax
import jax.numpy as jnp
from jax import lax
from jax.experimental import pallas as pl
from jax.experimental.pallas import tpu as pltpu
from jax.sharding import PartitionSpec as P

HEADS = 8
KB = 16
QB = 256
NY = 4
NZ = 8
NC = 8
D = 1024
HS = 128
ROWS = 512
SEGS = 512
REACH = 256
SCALE = 1.0 / math.sqrt(HS)
SCALE2 = SCALE * math.log2(math.e)
BF = jnp.bfloat16
F32 = jnp.float32
NT = (((1,), (1,)), ((), ()))
MESH = pl.DeviceIdType.MESH


def dot(a, b):
    return jnp.dot(a, b, preferred_element_type=F32)


def dot_nt(a, b):
    return lax.dot_general(a, b, NT, preferred_element_type=F32)


def normalize(x):
    return x * lax.rsqrt(jnp.mean(x * x, axis=-1, keepdims=True) + 1e-06)


OFFS = (0, -1, 1, -2, 2, -3, 3, 4)
COPIES = 31 + 63 + 95


def kernel(
    start_ref, end_ref, list_ref, tok_hbm, wqkv_hbm, wco_hbm, wkv2_hbm, att,
    tok, wqkv, wco, wkv2, scol, ecol, part, rc, rd, re, relay, red, rz, t1, t2, qkv, acc, mloc,
    lloc, qk, gath, kv2, load_sem, send_sem, recv_sem,
):
    c = lax.axis_index("coarse")
    f = lax.axis_index("fine")
    z = f // NY
    y = f % NY
    ya = y + 1 - 2 * (y % 2)
    yb = 3 - y
    yc = (y + 2) % 4
    up = (c + 1) % NC
    down = (c + NC - 1) % NC

    loads = [
        pltpu.make_async_copy(src, dst, load_sem.at[i])
        for i, (src, dst) in enumerate(
            ((tok_hbm, tok), (wqkv_hbm, wqkv), (wco_hbm, wco), (wkv2_hbm, wkv2))
        )
    ]
    for load in loads:
        load.start()

    at_y = lambda yy: {"fine": z * NY + yy}
    at_z = lambda zz: {"fine": zz * NY + y}
    at_c = lambda cc: {"coarse": cc}
    zat = lambda s: (z + s + NZ) % NZ

    barrier = pltpu.get_barrier_semaphore()
    peers = [at_z(zat(s)) for s in OFFS[1:]]
    peers += [at_y(ya), at_y(yb), at_c(up), at_c(down)]
    for peer in peers:
        pl.semaphore_signal(barrier, inc=1, device_id=peer, device_id_type=MESH)

    copies = []

    def send(src, dst, where):
        k = len(copies)
        copy = pltpu.make_async_remote_copy(
            src_ref=src, dst_ref=dst, send_sem=send_sem.at[k], recv_sem=recv_sem.at[k],
            device_id=where, device_id_type=MESH,
        )
        copy.start()
        copies.append(copy)
        return copy

    first_row = (c * (NY * NZ) + f) * ROWS
    ends = jnp.concatenate([start_ref[...] - first_row, end_ref[...] - first_row], axis=0).T
    for k in range(4):
        scol[2 * k:2 * k + 2] = ends[:, k:k + 1].reshape(2, NY, KB, 1)
        ecol[2 * k:2 * k + 2] = ends[:, k + 4:k + 5].reshape(2, NY, KB, 1)

    forward = lambda s: s in (0, -1, -2, -3)
    via = lambda s: yb if forward(s) else ya
    other = lambda s: ya if forward(s) else yb
    slot = {s: i for i, s in enumerate(OFFS)}
    waits = {}

    def member_sums(pair):
        low, high = [], []
        for s in pair:
            for yy in (y, other(s), via(s), yc):
                low.append(scol[zat(s), yy])
                high.append(ecol[zat(s), yy])
        low = jnp.concatenate(low, axis=0)
        high = jnp.concatenate(high, axis=0)
        place = lax.broadcasted_iota(jnp.int32, (128, ROWS), 1)
        member = jnp.where((place >= low) & (place < high), 1.0, 0.0).astype(BF)
        sums = dot(member, tok[...]).astype(BF)
        for i, s in enumerate(pair):
            part[slot[s]] = sums[i * 64:(i + 1) * 64].reshape(NY, KB, D)

    def spread(pair):
        for s in pair:
            k = slot[s]
            waits["c", s] = send(part.at[k, 3], rc.at[k], at_y(via(s)))
            waits["d", s] = send(part.at[k, 2], rd.at[k], at_y(via(s)))

    def pass_on(pair):
        for s in pair:
            k = slot[s]
            waits["c", s].wait_recv()
            relay[k] = (part[k, 1].astype(F32) + rc[k].astype(F32)).astype(BF)
            waits["e", s] = send(relay.at[k], re.at[k], at_y(other(s)))

    def settle(pair):
        for s in pair:
            k = slot[s]
            waits["d", s].wait_recv()
            waits["e", s].wait_recv()
            done = part[k, 0].astype(F32) + rd[k].astype(F32) + re[k].astype(F32)
            if s == 0:
                return done
            red[k] = done.astype(BF)
            waits["z", s] = send(red.at[k], rz.at[k], at_z(zat(s)))

    def project(j, carry):
        cols = pl.ds(pl.multiple_of(j * 256, 256), 256)
        qkv[:, cols] = dot(tok[...], wqkv[:, cols]).astype(BF)
        return carry

    def local(it, carry):
        rows = pl.ds(pl.multiple_of((it // HEADS) * QB, QB), QB)
        col = (it % HEADS) * HS
        cols = pl.ds(pl.multiple_of(col, HS), HS)
        keys = qkv[:, pl.ds(pl.multiple_of(col + D, HS), HS)]
        vals = qkv[:, pl.ds(pl.multiple_of(col + 2 * D, HS), HS)]
        s = dot_nt(qkv[rows, cols], keys)
        m = jnp.max(s, axis=1, keepdims=True)
        p = jnp.exp2((s - m) * SCALE2)
        lloc[it] = jnp.sum(p, axis=1, keepdims=True)
        mloc[it] = m
        acc[rows, cols] = dot(p.astype(BF), vals)
        return carry

    projects = lambda a, b: lax.fori_loop(a, b, project, 0)
    locals_ = lambda a, b: lax.fori_loop(a, b, local, 0)

    p0, p1, p2, p3 = (4, 3), (-3, 2), (-2, 1), (-1, 0)
    loads[0].wait()
    member_sums(p0)
    pl.semaphore_wait(barrier, len(peers))
    spread(p0)
    for pair in (p1, p2, p3):
        member_sums(pair)
        spread(pair)
    pass_on(p0)
    loads[1].wait()
    projects(0, 1)
    pass_on(p1)
    projects(1, 2)
    settle(p0)
    pass_on(p2)
    settle(p1)
    projects(2, 4)
    pass_on(p3)
    settle(p2)
    projects(4, 6)
    total = settle(p3)
    projects(6, 10)
    for s in OFFS[1:]:
        waits["z", s].wait_recv()
        total = total + rz[slot[s]].astype(F32)
    span = (ecol[z, y] - scol[z, y]).astype(F32)
    pooled = (total / jnp.sqrt(span)).astype(BF)
    t1[4 + z, y] = pooled

    def gather(table, base, halo, work):
        near, turn, hops, outs = {}, {}, {}, []

        def over(zb, yy):
            src = table.at[base + zb, yy]
            if halo:
                half = zb // 4
                spot = half * (zb - 4) + (1 - half) * (zb + 12)
                outs.append(send(src, table.at[spot, yy], at_c((c + 2 * half + NC - 1) % NC)))
            else:
                outs.append(send(src, table.at[zb, yy], at_c(up)))
                outs.append(send(src, table.at[zb + 16, yy], at_c(down)))

        def alike(zb, yy, where):
            return send(table.at[base + zb, yy], table.at[base + zb, yy], where)

        for s in OFFS[1:]:
            hops[-s if s != 4 else 4] = alike(z, y, at_z(zat(s)))
        for i in range(len(OFFS) + 4):
            if i < 8:
                s = OFFS[i]
                zb = zat(s)
                if s != 0:
                    hops[s].wait_recv()
                near[s] = (alike(zb, y, at_y(ya)), alike(zb, y, at_y(yb)))
                over(zb, y)
            if 2 <= i < 10:
                s = OFFS[i - 2]
                zb = zat(s)
                first, second = near[s]
                first.wait_recv()
                if forward(s):
                    turn[s] = alike(zb, ya, at_y(yb))
                over(zb, ya)
                second.wait_recv()
                if not forward(s):
                    turn[s] = alike(zb, yb, at_y(ya))
                over(zb, yb)
            if i >= 4:
                s = OFFS[i - 4]
                turn[s].wait_recv()
                over(zat(s), yc)
            if i in work:
                work[i]()
        for copy in outs:
            copy.wait_recv()

    def absorb():
        query = dot(pooled, wqkv[:, 0:D]).astype(BF)
        for h in range(HEADS):
            qk[h * KB:(h + 1) * KB] = dot_nt(
                query[:, h * HS:(h + 1) * HS], wqkv[:, D + h * HS:D + (h + 1) * HS]
            ).astype(BF)

    gather(
        t1, 4, True,
        {
            0: absorb,
            2: lambda: projects(10, 12),
            4: lambda: locals_(0, 2),
            7: lambda: locals_(2, 4),
            9: lambda: locals_(4, 6),
            11: lambda: locals_(6, 8),
        },
    )

    table = t1[...].reshape(1024, D)
    s = dot_nt(qk[...], table)
    row = lax.broadcasted_iota(jnp.int32, s.shape, 0) % KB + f * KB
    key = lax.broadcasted_iota(jnp.int32, s.shape, 1) - REACH
    s = jnp.where(jnp.abs(row - key) <= REACH, s, -1e30)
    m = jnp.max(s, axis=1, keepdims=True)
    p = jnp.exp2((s - m) * SCALE2)
    w = (p / jnp.sum(p, axis=1, keepdims=True)).astype(BF)
    mixed = dot(w, table).astype(BF)
    mix = jnp.concatenate(
        [
            dot(mixed[h * KB:(h + 1) * KB], wqkv[:, 2 * D + h * HS:2 * D + (h + 1) * HS])
            for h in range(HEADS)
        ],
        axis=1,
    ).astype(BF)
    loads[2].wait()
    state = normalize(dot(mix, wco[...])).astype(BF)
    t2[8 + z, y] = state
    gather(
        t2, 8, False,
        {
            1: lambda: locals_(8, 10),
            5: lambda: locals_(10, 12),
            9: lambda: locals_(12, 14),
            11: lambda: locals_(14, 16),
        },
    )

    for n in range(2):
        for j in range(8):
            rel = jnp.minimum((list_ref[n, j] - (c - 1) * 32 + 512) % 256, 95)
            k = n * 8 + j
            gath[k * KB:(k + 1) * KB] = t2[rel // NY, rel % NY]
    loads[3].wait()

    def second(j, carry):
        cols = pl.ds(pl.multiple_of(j * 256, 256), 256)
        kv2[:, cols] = dot(gath[...], wkv2[:, cols]).astype(BF)
        return carry

    lax.fori_loop(0, 8, second, 0)

    def remote(it, carry):
        n = it // HEADS
        rows = pl.ds(pl.multiple_of(n * QB, QB), QB)
        col = (it % HEADS) * HS
        cols = pl.ds(pl.multiple_of(col, HS), HS)
        listed = pl.ds(pl.multiple_of(n * 128, 128), 128)
        s = dot_nt(qkv[rows, cols], kv2[listed, cols])
        m0 = mloc[it]
        m = jnp.maximum(m0, jnp.max(s, axis=1, keepdims=True))
        a = jnp.exp2((m0 - m) * SCALE2)
        p = jnp.exp2((s - m) * SCALE2)
        total = a * lloc[it] + jnp.sum(p, axis=1, keepdims=True)
        vals = kv2[listed, pl.ds(pl.multiple_of(col + D, HS), HS)]
        o = acc[rows, cols] * a + dot(p.astype(BF), vals)
        att[rows, cols] = (o / total).astype(BF)
        return carry

    lax.fori_loop(0, 16, remote, 0, unroll=2)
    for copy in copies:
        copy.wait_send()


def body(tokens, w_qkv, w_coarse_out, w_kv2, w_out, seg_start, seg_end, block_lists):
    vmem = lambda shape, kind: pltpu.VMEM(shape, kind)
    attended = pl.pallas_call(
        kernel,
        out_shape=jax.ShapeDtypeStruct((ROWS, D), BF),
        in_specs=[
            pl.BlockSpec(memory_space=pltpu.VMEM),
            pl.BlockSpec(memory_space=pltpu.VMEM),
            pl.BlockSpec(memory_space=pltpu.SMEM),
        ] + [pl.BlockSpec(memory_space=pltpu.HBM)] * 4,
        out_specs=pl.BlockSpec(memory_space=pltpu.VMEM),
        scratch_shapes=[
            vmem((ROWS, D), BF),
            vmem((D, 3 * D), BF),
            vmem((D, D), BF),
            vmem((D, 2 * D), BF),
            vmem((NZ, NY, KB, 1), jnp.int32),
            vmem((NZ, NY, KB, 1), jnp.int32),
            vmem((NZ, NY, KB, D), BF),
            vmem((NZ, KB, D), BF),
            vmem((NZ, KB, D), BF),
            vmem((NZ, KB, D), BF),
            vmem((NZ, KB, D), BF),
            vmem((NZ, KB, D), BF),
            vmem((NZ, KB, D), BF),
            vmem((16, NY, KB, D), BF),
            vmem((24, NY, KB, D), BF),
            vmem((ROWS, 3 * D), BF),
            vmem((ROWS, D), F32),
            vmem((16, QB, 1), F32),
            vmem((16, QB, 1), F32),
            vmem((HEADS * KB, D), BF),
            vmem((256, D), BF),
            vmem((256, 2 * D), BF),
            pltpu.SemaphoreType.DMA((4,)),
            pltpu.SemaphoreType.DMA((COPIES,)),
            pltpu.SemaphoreType.DMA((COPIES,)),
        ],
        compiler_params=pltpu.CompilerParams(
            collective_id=0, has_side_effects=True, vmem_limit_bytes=60 * 1024 * 1024
        ),
    )(
        seg_start.reshape(4, 128), seg_end.reshape(4, 128), block_lists,
        tokens, w_qkv, w_coarse_out, w_kv2,
    )
    return normalize(dot(attended, w_out)).astype(BF)


def solution(mesh):
    placed = (
        P(("coarse", "fine"), None),
        P(),
        P(),
        P(),
        P(),
        P("coarse"),
        P("coarse"),
        P(("coarse", "fine"), None),
    )
    return jax.shard_map(
        body, mesh=mesh, in_specs=placed, out_specs=P(("coarse", "fine"), None), check_vma=False
    )
```

time: 97.1 us -> 89.4 us (0.921)
  local copies, waits for them, and re-layouts: 4.85 us -> 0.01 us
  Pallas kernels: 90.4 us -> 85.6 us
  matrix products: 0 us -> 2.56 us
    pallas_call x1, Pallas kernels: 90.4 us -> 85.6 us  [body(): pl.pallas_call(kernel, out_shape=jax.ShapeDtypeStruct((ROWS, D), BF), in_...]
    dot_general x0 -> x1, matrix products: none -> 2.56 us  [dot(): return jnp.dot(a, b, preferred_element_type=F32)]
    unnamed x1 -> x2, local copies, waits for them, and re-layouts: 2.26 us -> 0.01 us
    another operation x2 -> x0, local copies, waits for them, and re-layouts: 1.54 us -> none  [body(): seg = jnp.stack([seg_start, seg_end], axis=1).reshape(NZ, NY, KB, 2)]
    convert_element_type x0 -> x1, other arithmetic: none -> 1.16 us  [body(): return normalize(dot(attended, w_out)).astype(BF)]
where the time goes in v2:
time: 89.4 us; the launch traced here: 89.3 us
  Pallas kernels  85.6 us (96%)
  matrix products  2.56 us (3%)
  other arithmetic  1.17 us (1%)
    pallas_call x1, Pallas kernels, body(): pl.pallas_call(kernel, out_shape=jax.ShapeDtypeStruct((ROWS, D), BF), in_...  85.6 us
    dot_general x1, matrix products, dot(): return jnp.dot(a, b, preferred_element_type=F32)  2.56 us

profile of v2, /device:TPU:1, one launch (start us, length us, event | category | flops | bytes accessed | tf_op | source)
XLA Modules:
  0.0 89.3 jit_solution(6512510626194374936)
XLA Ops:
  0.0 0.0 copy-start
  0.0 85.6 %shard_map.82 = bf16[512,1024]{1,0:T(8,128)(2,1)} custom-call(s32[4,128]{1,0:T(4,128)} %bitcast.4, s32[4,128]{1,0:T(4,128)} %bitcast.5, s32[2,8]{1,0:T(2,128)} %list_ref.1, bf16[512,1024]{1,0:T(8,128)(2,1)} %tok_hbm.1, bf16[1024,3072]{1,0:T(8,128)(2,1)} %wqkv_hbm.1, bf16[1024,1024]{1,0:T(8,128)(2,1)} %wco_hbm.1, bf16[1024,2048]{1,0:T(8,128)(2,1)} %wkv2_hbm.1), custom_call_target="tpu_custom_call" | custom-call | tf_op jit(solution)/shard_map/pallas_call | solution.py:326
  85.6 0.0 copy-done
  85.6 2.6 %multiply_reduce_fusion = (f32[512]{0:T(512)S(1)}, f32[512,1024]{1,0:T(8,128)S(1)}) fusion(bf16[512,1024]{1,0:T(8,128)(2,1)} %shard_map.82, bf16[1024,1024]{1,0:T(8,128)(2,1)S(1)} %copy-done), kind=kOutput, calls=%fused_computation.1 | convolution fusion | flops 1074789888 | bytes 5244928 | tf_op jit(solution)/shard_map/dot_general | solution.py:30
  88.2 1.2 %multiply_convert_fusion = bf16[512,1024]{1,0:T(8,128)(2,1)} fusion(f32[512,1024]{1,0:T(8,128)S(1)} %get-tuple-element.6, f32[512]{0:T(512)S(1)} %add_rsqrt_fusion), kind=kLoop, calls=%fused_computation | loop fusion | flops 1048576 | bytes 3147776 | tf_op jit(solution)/shard_map/convert_element_type | solution.py:369
  (1 shorter events, 0.0 us)
Async XLA Ops:
  0.0 85.6 %copy-start = (bf16[1024,1024]{1,0:T(8,128)(2,1)S(1)}, bf16[1024,1024]{1,0:T(8,128)(2,1)}, u32[]{:S(2)}) copy-start(bf16[1024,1024]{1,0:T(8,128)(2,1)} %param.12) | copy-start | bytes 6291460

commit v3 on v2

--- a/solution.py
+++ b/solution.py
@@ -39,13 +39,13 @@
 
 
 OFFS = (0, -1, 1, -2, 2, -3, 3, 4)
-COPIES = 31 + 63 + 95
+COPIES = 31 + 24 + 95
 
 
 def kernel(
-    start_ref, end_ref, list_ref, tok_hbm, wqkv_hbm, wco_hbm, wkv2_hbm, att,
-    tok, wqkv, wco, wkv2, scol, ecol, part, rc, rd, re, relay, red, rz, t1, t2, qkv, acc, mloc,
-    lloc, qk, gath, kv2, load_sem, send_sem, recv_sem,
+    start_ref, end_ref, list_ref, tok_hbm, wqkv_hbm, wco_hbm, wkv2_hbm, wout_hbm,
+    out_ref, tok, wqkv, wco, wkv2, wout, scol, ecol, part, rc, rd, re, relay, red, rz, t1, tq, po, pm, go, gm, t2, qkv, acc,
+    mloc, lloc, qk, gath, kv2, att, load_sem, send_sem, recv_sem,
 ):
     c = lax.axis_index("coarse")
     f = lax.axis_index("fine")
@@ -60,7 +60,7 @@
     loads = [
         pltpu.make_async_copy(src, dst, load_sem.at[i])
         for i, (src, dst) in enumerate(
-            ((tok_hbm, tok), (wqkv_hbm, wqkv), (wco_hbm, wco), (wkv2_hbm, wkv2))
+            ((tok_hbm, tok), (wqkv_hbm, wqkv), (wco_hbm, wco), (wkv2_hbm, wkv2), (wout_hbm, wout))
         )
     ]
     for load in loads:
@@ -73,7 +73,7 @@
 
     barrier = pltpu.get_barrier_semaphore()
     peers = [at_z(zat(s)) for s in OFFS[1:]]
-    peers += [at_y(ya), at_y(yb), at_c(up), at_c(down)]
+    peers += [at_y(ya), at_y(yb), at_y(yc), at_c(up), at_c(down)]
     for peer in peers:
         pl.semaphore_signal(barrier, inc=1, device_id=peer, device_id_type=MESH)
 
@@ -119,7 +119,6 @@
         for s in pair:
             k = slot[s]
             waits["c", s] = send(part.at[k, 3], rc.at[k], at_y(via(s)))
-            waits["d", s] = send(part.at[k, 2], rd.at[k], at_y(via(s)))
 
     def pass_on(pair):
         for s in pair:
@@ -127,6 +126,9 @@
             waits["c", s].wait_recv()
             relay[k] = (part[k, 1].astype(F32) + rc[k].astype(F32)).astype(BF)
             waits["e", s] = send(relay.at[k], re.at[k], at_y(other(s)))
+        for s in pair:
+            k = slot[s]
+            waits["d", s] = send(part.at[k, 2], rd.at[k], at_y(via(s)))
 
     def settle(pair):
         for s in pair:
@@ -161,113 +163,109 @@
     projects = lambda a, b: lax.fori_loop(a, b, project, 0)
     locals_ = lambda a, b: lax.fori_loop(a, b, local, 0)
 
-    p0, p1, p2, p3 = (4, 3), (-3, 2), (-2, 1), (-1, 0)
+    pairs = (4, 3), (-3, 2), (-2, 1), (-1, 0)
     loads[0].wait()
-    member_sums(p0)
+    for pair in pairs:
+        member_sums(pair)
     pl.semaphore_wait(barrier, len(peers))
-    spread(p0)
-    for pair in (p1, p2, p3):
-        member_sums(pair)
+    for pair in pairs:
         spread(pair)
-    pass_on(p0)
     loads[1].wait()
-    projects(0, 1)
-    pass_on(p1)
-    projects(1, 2)
-    settle(p0)
-    pass_on(p2)
-    settle(p1)
-    projects(2, 4)
-    pass_on(p3)
-    settle(p2)
-    projects(4, 6)
-    total = settle(p3)
-    projects(6, 10)
+    projects(0, 3)
+    pass_on(pairs[0])
+    pass_on(pairs[1])
+    projects(3, 4)
+    settle(pairs[0])
+    pass_on(pairs[2])
+    projects(4, 5)
+    settle(pairs[1])
+    pass_on(pairs[3])
+    projects(5, 7)
+    settle(pairs[2])
+    projects(7, 9)
+    total = settle(pairs[3])
+    projects(9, 12)
     for s in OFFS[1:]:
         waits["z", s].wait_recv()
         total = total + rz[slot[s]].astype(F32)
     span = (ecol[z, y] - scol[z, y]).astype(F32)
     pooled = (total / jnp.sqrt(span)).astype(BF)
-    t1[4 + z, y] = pooled
-
-    def gather(table, base, halo, work):
-        near, turn, hops, outs = {}, {}, {}, []
-
-        def over(zb, yy):
-            src = table.at[base + zb, yy]
-            if halo:
-                half = zb // 4
-                spot = half * (zb - 4) + (1 - half) * (zb + 12)
-                outs.append(send(src, table.at[spot, yy], at_c((c + 2 * half + NC - 1) % NC)))
-            else:
-                outs.append(send(src, table.at[zb, yy], at_c(up)))
-                outs.append(send(src, table.at[zb + 16, yy], at_c(down)))
-
-        def alike(zb, yy, where):
-            return send(table.at[base + zb, yy], table.at[base + zb, yy], where)
-
-        for s in OFFS[1:]:
-            hops[-s if s != 4 else 4] = alike(z, y, at_z(zat(s)))
-        for i in range(len(OFFS) + 4):
-            if i < 8:
-                s = OFFS[i]
-                zb = zat(s)
-                if s != 0:
-                    hops[s].wait_recv()
-                near[s] = (alike(zb, y, at_y(ya)), alike(zb, y, at_y(yb)))
-                over(zb, y)
-            if 2 <= i < 10:
-                s = OFFS[i - 2]
-                zb = zat(s)
-                first, second = near[s]
-                first.wait_recv()
-                if forward(s):
-                    turn[s] = alike(zb, ya, at_y(yb))
-                over(zb, ya)
-                second.wait_recv()
-                if not forward(s):
-                    turn[s] = alike(zb, yb, at_y(ya))
-                over(zb, yb)
-            if i >= 4:
-                s = OFFS[i - 4]
-                turn[s].wait_recv()
-                over(zat(s), yc)
-            if i in work:
-                work[i]()
-        for copy in outs:
-            copy.wait_recv()
-
-    def absorb():
-        query = dot(pooled, wqkv[:, 0:D]).astype(BF)
-        for h in range(HEADS):
-            qk[h * KB:(h + 1) * KB] = dot_nt(
-                query[:, h * HS:(h + 1) * HS], wqkv[:, D + h * HS:D + (h + 1) * HS]
-            ).astype(BF)
-
-    gather(
-        t1, 4, True,
-        {
-            0: absorb,
-            2: lambda: projects(10, 12),
-            4: lambda: locals_(0, 2),
-            7: lambda: locals_(2, 4),
-            9: lambda: locals_(4, 6),
-            11: lambda: locals_(6, 8),
-        },
-    )
-
-    table = t1[...].reshape(1024, D)
+    t1[4 + z] = pooled
+    tq[y] = pooled
+
+    def across(zb):
+        half = zb // 4
+        spot = half * (zb - 4) + (1 - half) * (zb + 12)
+        return send(t1.at[4 + zb], t1.at[spot], at_c((c + 2 * half + NC - 1) % NC))
+
+    hops = {}
+    rows_in = []
+    for s in (1, -1, 4, 3, -3, 2, -2):
+        hops[-s if s != 4 else 4] = send(t1.at[4 + z], t1.at[4 + z], at_z(zat(s)))
+    for yy in (yc, ya, yb):
+        rows_in.append(send(tq.at[y], tq.at[y], at_y(yy)))
+    halo = [across(z)]
+    for copy in rows_in:
+        copy.wait_recv()
+
+    query = dot(tq[...].reshape(64, D), wqkv[:, 0:D]).astype(BF)
+
+    def absorb(h):
+        qk[h * 64:(h + 1) * 64] = dot_nt(
+            query[:, h * HS:(h + 1) * HS], wqkv[:, D + h * HS:D + (h + 1) * HS]
+        ).astype(BF)
+
+    absorb(0)
+    absorb(1)
+    for i, s in enumerate((-1, 1, -2, 2, -3, 3, 4)):
+        hops[s].wait_recv()
+        halo.append(across(zat(s)))
+        if i < 6:
+            absorb(2 + i)
+    locals_(0, 5)
+    for copy in halo:
+        copy.wait_recv()
+
+    table = t1[...].reshape(256, D)
     s = dot_nt(qk[...], table)
-    row = lax.broadcasted_iota(jnp.int32, s.shape, 0) % KB + f * KB
-    key = lax.broadcasted_iota(jnp.int32, s.shape, 1) - REACH
+    row = z * 64 + lax.broadcasted_iota(jnp.int32, s.shape, 0) % 64
+    place = lax.broadcasted_iota(jnp.int32, s.shape, 1)
+    key = place // KB * 64 + place % KB + y * KB - REACH
     s = jnp.where(jnp.abs(row - key) <= REACH, s, -1e30)
     m = jnp.max(s, axis=1, keepdims=True)
     p = jnp.exp2((s - m) * SCALE2)
-    w = (p / jnp.sum(p, axis=1, keepdims=True)).astype(BF)
-    mixed = dot(w, table).astype(BF)
+    l = jnp.sum(p, axis=1, keepdims=True)
+    mixed = dot(p.astype(BF), table).astype(BF)
+    lane = lax.broadcasted_iota(jnp.int32, (64, HS), 1)
+    tops = jnp.zeros((64, HS), F32)
+    sums = jnp.ones((64, HS), F32)
+    for h in range(HEADS):
+        rows = slice(h * 64, (h + 1) * 64)
+        tops = jnp.where(lane == h, m[rows], tops)
+        sums = jnp.where(lane == h, l[rows], sums)
+        cols = slice(2 * D + h * HS, 2 * D + (h + 1) * HS)
+        po[:, :, h * HS:(h + 1) * HS] = dot(mixed[rows], wqkv[:, cols]).astype(BF).reshape(
+            NY, KB, HS
+        )
+    pm[:, 0] = tops.reshape(NY, KB, HS)
+    pm[:, 1] = sums.reshape(NY, KB, HS)
+    parts = []
+    for j, yy in enumerate((yc, ya, yb)):
+        parts.append(send(pm.at[yy], gm.at[j], at_y(yy)))
+        parts.append(send(po.at[yy], go.at[j], at_y(yy)))
+    locals_(5, 7)
+    for copy in parts:
+        copy.wait_recv()
+    tops = [pm[y, 0]] + [gm[j, 0] for j in range(3)]
+    sums = [pm[y, 1]] + [gm[j, 1] for j in range(3)]
+    outs = [po[y].astype(F32)] + [go[j].astype(F32) for j in range(3)]
+    peak = jnp.maximum(jnp.maximum(tops[0], tops[1]), jnp.maximum(tops[2], tops[3]))
+    shares = [jnp.exp2((t - peak) * SCALE2) for t in tops]
+    whole = sum(a * b for a, b in zip(shares, sums))
+    shares = [a / whole for a in shares]
     mix = jnp.concatenate(
         [
-            dot(mixed[h * KB:(h + 1) * KB], wqkv[:, 2 * D + h * HS:2 * D + (h + 1) * HS])
+            sum(a[:, h:h + 1] * o[:, h * HS:(h + 1) * HS] for a, o in zip(shares, outs))
             for h in range(HEADS)
         ],
         axis=1,
@@ -275,15 +273,51 @@
     loads[2].wait()
     state = normalize(dot(mix, wco[...])).astype(BF)
     t2[8 + z, y] = state
-    gather(
-        t2, 8, False,
-        {
-            1: lambda: locals_(8, 10),
-            5: lambda: locals_(10, 12),
-            9: lambda: locals_(12, 14),
-            11: lambda: locals_(14, 16),
-        },
-    )
+    near, turn, hops, halo = {}, {}, {}, []
+
+    def over(zb, yy):
+        src = t2.at[8 + zb, yy]
+        halo.append(send(src, t2.at[zb, yy], at_c(up)))
+        halo.append(send(src, t2.at[zb + 16, yy], at_c(down)))
+
+    def alike(zb, yy, where):
+        return send(t2.at[8 + zb, yy], t2.at[8 + zb, yy], where)
+
+    def event(kind, s):
+        zb = zat(s)
+        if kind == "z":
+            if s != 0:
+                hops[s].wait_recv()
+            near[s] = (alike(zb, y, at_y(ya)), alike(zb, y, at_y(yb)))
+            over(zb, y)
+        elif kind == "y":
+            first, second = near[s]
+            first.wait_recv()
+            if forward(s):
+                turn[s] = alike(zb, ya, at_y(yb))
+            second.wait_recv()
+            if not forward(s):
+                turn[s] = alike(zb, yb, at_y(ya))
+            over(zb, ya)
+            over(zb, yb)
+        elif kind == "c":
+            turn[s].wait_recv()
+            over(zb, yc)
+        else:
+            locals_(s, s + 1)
+
+    for s in (1, -1, 4, 3, -3, 2, -2):
+        hops[-s if s != 4 else 4] = alike(z, y, at_z(zat(s)))
+    for kind, s in (
+        ("z", 0), ("w", 7), ("w", 8), ("w", 9), ("w", 10), ("y", 0), ("z", -1), ("z", 1),
+        ("w", 11), ("z", -2), ("z", 2), ("w", 12), ("c", 0), ("z", -3), ("z", 3), ("z", 4),
+        ("y", -1), ("y", 1), ("w", 13), ("y", -2), ("y", 2), ("c", -1), ("c", 1), ("y", -3),
+        ("y", 3), ("w", 14), ("c", -2), ("c", 2), ("y", 4), ("c", -3), ("c", 3), ("w", 15),
+        ("c", 4),
+    ):
+        event(kind, s)
+    for copy in halo:
+        copy.wait_recv()
 
     for n in range(2):
         for j in range(8):
@@ -316,27 +350,36 @@
         att[rows, cols] = (o / total).astype(BF)
         return carry
 
-    lax.fori_loop(0, 16, remote, 0, unroll=2)
+    lax.fori_loop(0, 16, remote, 0, unroll=4)
+    loads[4].wait()
+
+    def finish(i, carry):
+        rows = pl.ds(pl.multiple_of(i * 128, 128), 128)
+        out_ref[rows, :] = normalize(dot(att[rows, :], wout[...])).astype(BF)
+        return carry
+
+    lax.fori_loop(0, 4, finish, 0)
     for copy in copies:
         copy.wait_send()
 
 
 def body(tokens, w_qkv, w_coarse_out, w_kv2, w_out, seg_start, seg_end, block_lists):
     vmem = lambda shape, kind: pltpu.VMEM(shape, kind)
-    attended = pl.pallas_call(
+    return pl.pallas_call(
         kernel,
         out_shape=jax.ShapeDtypeStruct((ROWS, D), BF),
         in_specs=[
             pl.BlockSpec(memory_space=pltpu.VMEM),
             pl.BlockSpec(memory_space=pltpu.VMEM),
             pl.BlockSpec(memory_space=pltpu.SMEM),
-        ] + [pl.BlockSpec(memory_space=pltpu.HBM)] * 4,
+        ] + [pl.BlockSpec(memory_space=pltpu.HBM)] * 5,
         out_specs=pl.BlockSpec(memory_space=pltpu.VMEM),
         scratch_shapes=[
             vmem((ROWS, D), BF),
             vmem((D, 3 * D), BF),
             vmem((D, D), BF),
             vmem((D, 2 * D), BF),
+            vmem((D, D), BF),
             vmem((NZ, NY, KB, 1), jnp.int32),
             vmem((NZ, NY, KB, 1), jnp.int32),
             vmem((NZ, NY, KB, D), BF),
@@ -346,27 +389,32 @@
             vmem((NZ, KB, D), BF),
             vmem((NZ, KB, D), BF),
             vmem((NZ, KB, D), BF),
-            vmem((16, NY, KB, D), BF),
+            vmem((16, KB, D), BF),
+            vmem((NY, KB, D), BF),
+            vmem((NY, KB, D), BF),
+            vmem((NY, 2, KB, HS), F32),
+            vmem((3, KB, D), BF),
+            vmem((3, 2, KB, HS), F32),
             vmem((24, NY, KB, D), BF),
             vmem((ROWS, 3 * D), BF),
             vmem((ROWS, D), F32),
             vmem((16, QB, 1), F32),
             vmem((16, QB, 1), F32),
-            vmem((HEADS * KB, D), BF),
+            vmem((HEADS * 64, D), BF),
             vmem((256, D), BF),
             vmem((256, 2 * D), BF),
-            pltpu.SemaphoreType.DMA((4,)),
+            vmem((ROWS, D), BF),
+            pltpu.SemaphoreType.DMA((5,)),
             pltpu.SemaphoreType.DMA((COPIES,)),
             pltpu.SemaphoreType.DMA((COPIES,)),
         ],
         compiler_params=pltpu.CompilerParams(
-            collective_id=0, has_side_effects=True, vmem_limit_bytes=60 * 1024 * 1024
+            collective_id=0, has_side_effects=True, vmem_limit_bytes=54 * 1024 * 1024
         ),
     )(
         seg_start.reshape(4, 128), seg_end.reshape(4, 128), block_lists,
-        tokens, w_qkv, w_coarse_out, w_kv2,
+        tokens, w_qkv, w_coarse_out, w_kv2, w_out,
     )
-    return normalize(dot(attended, w_out)).astype(BF)
 
 
 def solution(mesh):

time: 89.4 us -> 81.8 us (0.915)
  Pallas kernels: 85.6 us -> 79.4 us
  matrix products: 2.56 us -> 0 us
  local copies, waits for them, and re-layouts: 0.01 us -> 2.26 us
  other arithmetic: 1.17 us -> 0 us
    pallas_call x1, Pallas kernels: 85.6 us -> 79.4 us  [body(): pl.pallas_call(kernel, out_shape=jax.ShapeDtypeStruct((ROWS, D), BF), in_...]
    dot_general x1 -> x0, matrix products: 2.56 us -> none  [dot(): return jnp.dot(a, b, preferred_element_type=F32)]
    unnamed x2 -> x1, local copies, waits for them, and re-layouts: 0.01 us -> 2.26 us
    convert_element_type x1 -> x0, other arithmetic: 1.16 us -> none  [body(): return normalize(dot(attended, w_out)).astype(BF)]
where the time goes in v3:
time: 81.8 us; the launch traced here: 81.6 us
  Pallas kernels  79.4 us (97%)
  local copies, waits for them, and re-layouts  2.26 us (3%)
    pallas_call x1, Pallas kernels, body(): pl.pallas_call(kernel, out_shape=jax.ShapeDtypeStruct((ROWS, D), BF), in_...  79.4 us
    unnamed x1, local copies, waits for them, and re-layouts  2.26 us

profile of v3, /device:TPU:1, one launch (start us, length us, event | category | flops | bytes accessed | tf_op | source)
XLA Modules:
  0.0 81.6 jit_solution(11057814738319921543)
XLA Ops:
  0.0 79.4 %shard_map.82 = bf16[512,1024]{1,0:T(8,128)(2,1)} custom-call(s32[4,128]{1,0:T(4,128)} %bitcast.2, s32[4,128]{1,0:T(4,128)} %bitcast.3, s32[2,8]{1,0:T(2,128)} %list_ref.1, bf16[512,1024]{1,0:T(8,128)(2,1)} %tok_hbm.1, bf16[1024,3072]{1,0:T(8,128)(2,1)} %wqkv_hbm.1, bf16[1024,1024]{1,0:T(8,128)(2,1)} %wco_hbm.1, bf16[1024,2048]{1,0:T(8,128)(2,1)} %wkv2_hbm.1, ...), custom_call_target="tpu_custom_call" | custom-call | tf_op jit(solution)/shard_map/pallas_call | solution.py:368
  79.4 2.3 %copy.10 = bf16[512,1024]{1,0:T(8,128)(2,1)} copy(bf16[512,1024]{1,0:T(8,128)(2,1)} %shard_map.82) | data formatting | bytes 2097152

commit v4 on v3

--- a/solution.py
+++ b/solution.py
@@ -63,8 +63,7 @@
             ((tok_hbm, tok), (wqkv_hbm, wqkv), (wco_hbm, wco), (wkv2_hbm, wkv2), (wout_hbm, wout))
         )
     ]
-    for load in loads:
-        load.start()
+    loads[0].start()
 
     at_y = lambda yy: {"fine": z * NY + yy}
     at_z = lambda zz: {"fine": zz * NY + y}
@@ -155,8 +154,8 @@
         s = dot_nt(qkv[rows, cols], keys)
         m = jnp.max(s, axis=1, keepdims=True)
         p = jnp.exp2((s - m) * SCALE2)
-        lloc[it] = jnp.sum(p, axis=1, keepdims=True)
-        mloc[it] = m
+        lloc[it] = jnp.broadcast_to(jnp.sum(p, axis=1, keepdims=True), (QB, HS))
+        mloc[it] = jnp.broadcast_to(m, (QB, HS))
         acc[rows, cols] = dot(p.astype(BF), vals)
         return carry
 
@@ -165,6 +164,8 @@
 
     pairs = (4, 3), (-3, 2), (-2, 1), (-1, 0)
     loads[0].wait()
+    for load in loads[1:]:
+        load.start()
     for pair in pairs:
         member_sums(pair)
     pl.semaphore_wait(barrier, len(peers))
@@ -347,18 +348,18 @@
         total = a * lloc[it] + jnp.sum(p, axis=1, keepdims=True)
         vals = kv2[listed, pl.ds(pl.multiple_of(col + D, HS), HS)]
         o = acc[rows, cols] * a + dot(p.astype(BF), vals)
-        att[rows, cols] = (o / total).astype(BF)
+        att[rows, cols] = (o * (1.0 / total)).astype(BF)
         return carry
 
-    lax.fori_loop(0, 16, remote, 0, unroll=4)
+    lax.fori_loop(0, 16, remote, 0, unroll=8)
     loads[4].wait()
 
     def finish(i, carry):
-        rows = pl.ds(pl.multiple_of(i * 128, 128), 128)
+        rows = pl.ds(pl.multiple_of(i * 256, 256), 256)
         out_ref[rows, :] = normalize(dot(att[rows, :], wout[...])).astype(BF)
         return carry
 
-    lax.fori_loop(0, 4, finish, 0)
+    lax.fori_loop(0, 2, finish, 0)
     for copy in copies:
         copy.wait_send()
 
@@ -398,8 +399,8 @@
             vmem((24, NY, KB, D), BF),
             vmem((ROWS, 3 * D), BF),
             vmem((ROWS, D), F32),
-            vmem((16, QB, 1), F32),
-            vmem((16, QB, 1), F32),
+            vmem((16, QB, HS), F32),
+            vmem((16, QB, HS), F32),
             vmem((HEADS * 64, D), BF),
             vmem((256, D), BF),
             vmem((256, 2 * D), BF),

time: 81.8 us -> 77.6 us (0.949)
  Pallas kernels: 79.4 us -> 75.2 us
    pallas_call x1, Pallas kernels: 79.4 us -> 75.2 us  [body(): pl.pallas_call(kernel, out_shape=jax.ShapeDtypeStruct((ROWS, D), BF), in_...]
where the time goes in v4:
time: 77.6 us; the launch traced here: 77.5 us
  Pallas kernels  75.2 us (97%)
  local copies, waits for them, and re-layouts  2.26 us (3%)
    pallas_call x1, Pallas kernels, body(): pl.pallas_call(kernel, out_shape=jax.ShapeDtypeStruct((ROWS, D), BF), in_...  75.2 us
    unnamed x1, local copies, waits for them, and re-layouts  2.26 us

profile of v4, /device:TPU:1, one launch (start us, length us, event | category | flops | bytes accessed | tf_op | source)
XLA Modules:
  0.0 77.5 jit_solution(4152150482434151593)
XLA Ops:
  0.0 75.2 %shard_map.82 = bf16[512,1024]{1,0:T(8,128)(2,1)} custom-call(s32[4,128]{1,0:T(4,128)} %bitcast.2, s32[4,128]{1,0:T(4,128)} %bitcast.3, s32[2,8]{1,0:T(2,128)} %list_ref.1, bf16[512,1024]{1,0:T(8,128)(2,1)} %tok_hbm.1, bf16[1024,3072]{1,0:T(8,128)(2,1)} %wqkv_hbm.1, bf16[1024,1024]{1,0:T(8,128)(2,1)} %wco_hbm.1, bf16[1024,2048]{1,0:T(8,128)(2,1)} %wkv2_hbm.1, ...), custom_call_target="tpu_custom_call" | custom-call | tf_op jit(solution)/shard_map/pallas_call | solution.py:369
  75.2 2.3 %copy.10 = bf16[512,1024]{1,0:T(8,128)(2,1)} copy(bf16[512,1024]{1,0:T(8,128)(2,1)} %shard_map.82) | data formatting | bytes 2097152

commit v5 on v4

--- a/solution.py
+++ b/solution.py
@@ -39,6 +39,7 @@
 
 
 OFFS = (0, -1, 1, -2, 2, -3, 3, 4)
+FAR = (-3, 3, 4)
 COPIES = 31 + 24 + 95
 
 
@@ -290,14 +291,16 @@
             if s != 0:
                 hops[s].wait_recv()
             near[s] = (alike(zb, y, at_y(ya)), alike(zb, y, at_y(yb)))
+            if s in FAR:
+                turn[s] = alike(zb, y, at_y(yc))
             over(zb, y)
         elif kind == "y":
             first, second = near[s]
             first.wait_recv()
-            if forward(s):
+            if forward(s) and s not in FAR:
                 turn[s] = alike(zb, ya, at_y(yb))
             second.wait_recv()
-            if not forward(s):
+            if not forward(s) and s not in FAR:
                 turn[s] = alike(zb, yb, at_y(ya))
             over(zb, ya)
             over(zb, yb)
@@ -410,7 +413,7 @@
             pltpu.SemaphoreType.DMA((COPIES,)),
         ],
         compiler_params=pltpu.CompilerParams(
-            collective_id=0, has_side_effects=True, vmem_limit_bytes=54 * 1024 * 1024
+            collective_id=0, has_side_effects=True, vmem_limit_bytes=52 * 1024 * 1024
         ),
     )(
         seg_start.reshape(4, 128), seg_end.reshape(4, 128), block_lists,

time: 77.6 us -> 77.9 us (level)
    unnamed x1 -> x7, local copies, waits for them, and re-layouts: 2.26 us -> 3.01 us
where the time goes in v5:
time: 77.9 us; the launch traced here: 77.7 us
  Pallas kernels  74.7 us (96%)
  local copies, waits for them, and re-layouts  3.01 us (4%)
    pallas_call x1, Pallas kernels, body(): pl.pallas_call(kernel, out_shape=jax.ShapeDtypeStruct((ROWS, D), BF), in_...  74.7 us
    unnamed x7, local copies, waits for them, and re-layouts  3.01 us

profile of v5, /device:TPU:1, one launch (start us, length us, event | category | flops | bytes accessed | tf_op | source)
XLA Modules:
  0.0 77.7 jit_solution(12217343275221415812)
XLA Ops:
  0.0 0.0 copy-start
  0.0 0.7 copy-done
  0.7 0.0 copy-start.1
  0.7 0.7 copy-done.1
  1.4 0.0 copy-start.2
  1.4 0.7 copy-done.2
  2.0 74.7 %shard_map.82 = bf16[512,1024]{1,0:T(8,128)(2,1)S(1)} custom-call(s32[4,128]{1,0:T(4,128)S(1)} %bitcast.2, s32[4,128]{1,0:T(4,128)S(1)} %bitcast.3, s32[2,8]{1,0:T(2,128)S(1)} %copy-done.2, bf16[512,1024]{1,0:T(8,128)(2,1)} %tok_hbm.1, bf16[1024,3072]{1,0:T(8,128)(2,1)} %wqkv_hbm.1, bf16[1024,1024]{1,0:T(8,128)(2,1)} %wco_hbm.1, ...), custom_call_target="tpu_custom_call" | custom-call | tf_op jit(solution)/shard_map/pallas_call | solution.py:372
  76.7 1.0 %copy.10 = bf16[512,1024]{1,0:T(8,128)(2,1)} copy(bf16[512,1024]{1,0:T(8,128)(2,1)S(1)} %shard_map.82) | data formatting | bytes 2097152
Async XLA Ops:
  0.0 0.7 copy-start
  0.7 0.7 copy-start.1
  1.4 0.7 copy-start.2

commit v6 on v4

--- a/solution.py
+++ b/solution.py
@@ -44,7 +44,7 @@
 
 def kernel(
     start_ref, end_ref, list_ref, tok_hbm, wqkv_hbm, wco_hbm, wkv2_hbm, wout_hbm,
-    out_ref, tok, wqkv, wco, wkv2, wout, scol, ecol, part, rc, rd, re, relay, red, rz, t1, tq, po, pm, go, gm, t2, qkv, acc,
+    out_ref, tok, wqkv, wco, wkv2, wout, scol, ecol, part, rc, rd, re, relay, red, rz, t1, vcol, tq, po, pm, go, gm, t2, qkv, acc,
     mloc, lloc, qk, gath, kv2, att, load_sem, send_sem, recv_sem,
 ):
     c = lax.axis_index("coarse")
@@ -223,12 +223,18 @@
         halo.append(across(zat(s)))
         if i < 6:
             absorb(2 + i)
-    locals_(0, 5)
+    half = (8, KB, D)
+    vcol[4:12] = dot(t1[4:12].reshape(128, D), wqkv[:, 2 * D:3 * D]).astype(BF).reshape(half)
+    locals_(0, 3)
     for copy in halo:
         copy.wait_recv()
 
     table = t1[...].reshape(256, D)
     s = dot_nt(qk[...], table)
+    edges = jnp.concatenate([table[0:64], table[192:256]], axis=0)
+    edges = dot(edges, wqkv[:, 2 * D:3 * D]).astype(BF)
+    vcol[0:4] = edges[0:64].reshape(4, KB, D)
+    vcol[12:16] = edges[64:128].reshape(4, KB, D)
     row = z * 64 + lax.broadcasted_iota(jnp.int32, s.shape, 0) % 64
     place = lax.broadcasted_iota(jnp.int32, s.shape, 1)
     key = place // KB * 64 + place % KB + y * KB - REACH
@@ -236,7 +242,8 @@
     m = jnp.max(s, axis=1, keepdims=True)
     p = jnp.exp2((s - m) * SCALE2)
     l = jnp.sum(p, axis=1, keepdims=True)
-    mixed = dot(p.astype(BF), table).astype(BF)
+    values = vcol[...].reshape(256, D)
+    p = p.astype(BF)
     lane = lax.broadcasted_iota(jnp.int32, (64, HS), 1)
     tops = jnp.zeros((64, HS), F32)
     sums = jnp.ones((64, HS), F32)
@@ -244,8 +251,8 @@
         rows = slice(h * 64, (h + 1) * 64)
         tops = jnp.where(lane == h, m[rows], tops)
         sums = jnp.where(lane == h, l[rows], sums)
-        cols = slice(2 * D + h * HS, 2 * D + (h + 1) * HS)
-        po[:, :, h * HS:(h + 1) * HS] = dot(mixed[rows], wqkv[:, cols]).astype(BF).reshape(
+        cols = slice(h * HS, (h + 1) * HS)
+        po[:, :, cols] = dot(p[rows], values[:, cols]).astype(BF).reshape(
             NY, KB, HS
         )
     pm[:, 0] = tops.reshape(NY, KB, HS)
@@ -254,7 +261,7 @@
     for j, yy in enumerate((yc, ya, yb)):
         parts.append(send(pm.at[yy], gm.at[j], at_y(yy)))
         parts.append(send(po.at[yy], go.at[j], at_y(yy)))
-    locals_(5, 7)
+    locals_(3, 7)
     for copy in parts:
         copy.wait_recv()
     tops = [pm[y, 0]] + [gm[j, 0] for j in range(3)]
@@ -328,11 +335,11 @@
     loads[3].wait()
 
     def second(j, carry):
-        cols = pl.ds(pl.multiple_of(j * 256, 256), 256)
+        cols = pl.ds(pl.multiple_of(j * 512, 512), 512)
         kv2[:, cols] = dot(gath[...], wkv2[:, cols]).astype(BF)
         return carry
 
-    lax.fori_loop(0, 8, second, 0)
+    lax.fori_loop(0, 4, second, 0)
 
     def remote(it, carry):
         n = it // HEADS
@@ -390,6 +397,7 @@
             vmem((NZ, KB, D), BF),
             vmem((NZ, KB, D), BF),
             vmem((NZ, KB, D), BF),
+            vmem((16, KB, D), BF),
             vmem((16, KB, D), BF),
             vmem((NY, KB, D), BF),
             vmem((NY, KB, D), BF),

time: 77.6 us -> 75.5 us (0.973)
  Pallas kernels: 75.2 us -> 73 us
    pallas_call x1, Pallas kernels: 75.2 us -> 73 us  [body(): pl.pallas_call(kernel, out_shape=jax.ShapeDtypeStruct((ROWS, D), BF), in_...]
where the time goes in v6:
time: 75.5 us; the launch traced here: 75.3 us
  Pallas kernels  73 us (97%)
  local copies, waits for them, and re-layouts  2.26 us (3%)
    pallas_call x1, Pallas kernels, body(): pl.pallas_call(kernel, out_shape=jax.ShapeDtypeStruct((ROWS, D), BF), in_...  73 us
    unnamed x1, local copies, waits for them, and re-layouts  2.26 us

profile of v6, /device:TPU:1, one launch (start us, length us, event | category | flops | bytes accessed | tf_op | source)
XLA Modules:
  0.0 75.3 jit_solution(3466368094939483656)
XLA Ops:
  0.0 73.0 %shard_map.82 = bf16[512,1024]{1,0:T(8,128)(2,1)} custom-call(s32[4,128]{1,0:T(4,128)} %bitcast.2, s32[4,128]{1,0:T(4,128)} %bitcast.3, s32[2,8]{1,0:T(2,128)} %list_ref.1, bf16[512,1024]{1,0:T(8,128)(2,1)} %tok_hbm.1, bf16[1024,3072]{1,0:T(8,128)(2,1)} %wqkv_hbm.1, bf16[1024,1024]{1,0:T(8,128)(2,1)} %wco_hbm.1, bf16[1024,2048]{1,0:T(8,128)(2,1)} %wkv2_hbm.1, ...), custom_call_target="tpu_custom_call" | custom-call | tf_op jit(solution)/shard_map/pallas_call | solution.py:376
  73.0 2.3 %copy.10 = bf16[512,1024]{1,0:T(8,128)(2,1)} copy(bf16[512,1024]{1,0:T(8,128)(2,1)} %shard_map.82) | data formatting | bytes 2097152
